TPU v7x, 256 devices: a whole 4x4x8 slice. The times are simulated.
256 devices in a mesh: gx: 16 (over x, y_lo, core), col: 16 (over y_hi, z).
Axes of the slice: x: 4, y: 4 (y_hi: 2, y_lo: 2; y = y_hi * 2 + y_lo), z: 8, core: 2. Of those that a mesh axis runs over, the one named last changes fastest.
Arguments:
- field: bfloat16 [32, 32, 128, 256], P('col', 'gx'), may hold values from -6 to 6
- kernel: bfloat16 [64, 32, 3, 3, 3], replicated, may hold values from -0.21875 to 0.21875
- bias: float32 [64], P('col'), may hold values from -3 to 3
- cotangent: bfloat16 [64, 16, 64, 128], P('col', 'gx'), may hold values from -6 to 6
Outputs:
- out_act: bfloat16 [64, 16, 64, 128], P('col', 'gx')
- in_grad: bfloat16 [32, 32, 128, 256], P('col', 'gx')
All inputs are finite; a program needn't handle non-finite values.
Results may differ from a plain program's by a relative error of at most 0.014.
Values may be sent and summed in bfloat16 or wider, within the bound.
A program may use at most 128 MiB of HBM per device.

v0:
```python
import functools

import jax
import jax.numpy as jnp
from jax import lax
from jax.experimental import pallas as pl
from jax.experimental.pallas import tpu as pltpu
from jax.sharding import PartitionSpec as P

F32 = jnp.float32
BF16 = jnp.bfloat16
MESH = pl.DeviceIdType.MESH

X1, X0, CT, BS, OS, G0, G1, XH, H1, HM, H0, M1, N0, N1 = range(14)
KINDS = 14


def iota(shape, dim):
    return lax.broadcasted_iota(jnp.int32, shape, dim)


def one_hot(hit):
    return jnp.where(hit, 1.0, 0.0).astype(BF16)


def dot(a, b):
    return jnp.dot(a, b, preferred_element_type=F32)


def row_block(position, ranks):
    return position + (position // (ranks // 2)) * (3 * ranks // 2 - 1 - 2 * position)


def block_kernel(
    slabs, ranks,
    field, wt, bias, cot,
    act, grad,
    rx1, rx0, rxh, h1, h0, hm, hs1, hs0,
    cs, crx, bs, brx, outs, orx, m0, m1, tg0, tg1,
    tf, tt, sel, send, recv,
):
    slab = lax.axis_index("gx")
    me = lax.axis_index("col")
    block = row_block(me, ranks)
    above = lax.rem(slab + 1, slabs)
    below = lax.rem(slab + slabs - 1, slabs)
    after = row_block(lax.rem(block + 1, ranks), ranks)
    before = row_block(lax.rem(block + ranks - 1, ranks), ranks)

    barrier = pltpu.get_barrier_semaphore()

    def greet(step, carry):
        peer = lax.rem(me + step, ranks)
        pl.semaphore_signal(barrier, inc=1, device_id=(slab, peer), device_id_type=MESH)
        return carry

    lax.fori_loop(1, ranks, greet, 0)
    for where in ((above, me), (below, me), (above, after), (below, before)):
        pl.semaphore_signal(barrier, inc=1, device_id=where, device_id_type=MESH)

    def remote(src, dst, kind, where):
        return pltpu.make_async_remote_copy(
            src_ref=src, dst_ref=dst, send_sem=send.at[kind], recv_sem=recv.at[kind],
            device_id=where, device_id_type=MESH,
        )

    def landed(ref, kind):
        pltpu.make_async_copy(ref, ref, recv.at[kind]).wait()

    def left(ref, kind):
        pltpu.make_async_copy(ref, ref, send.at[kind]).wait()

    def scatter(kind, source, target):
        def one(step, carry):
            peer = lax.rem(me + step, ranks)
            remote(source(peer), target, kind, (slab, peer)).start()
            return carry

        lax.fori_loop(1, ranks, one, 0)
        pltpu.make_async_copy(source(me), target, recv.at[kind]).start()

    to = iota((256, 256), 0)
    frm = iota((256, 256), 1)
    order = one_hot(frm == (to % 4) * 64 + (to // 16) * 4 + (to // 4) % 4)
    cs[...] = dot(order, cot[...]).astype(BF16).reshape(ranks, 16, 128)
    bs[...] = jnp.zeros(bs.shape, F32)
    bs[0:1, 0:4] = bias[...]
    source_z = iota((256, 384), 0)
    tap = iota((256, 384), 1)
    sel[...] = one_hot(source_z == (2 * (tap % 128) + tap // 128 + 255) % 256)

    pl.semaphore_wait(barrier, ranks - 1 + 4)

    scatter(X1, lambda peer: field.at[:, 1, row_block(peer, ranks)], rx1.at[me])
    scatter(X0, lambda peer: field.at[:, 0, row_block(peer, ranks)], rx0.at[me])
    scatter(CT, lambda peer: cs.at[row_block(peer, ranks)], crx.at[me])
    scatter(BS, lambda peer: bs, brx.at[me])

    spread_t = one_hot(iota((32, 256), 0) == iota((32, 256), 1) // 8)
    spread = one_hot(iota((256, 32), 1) == iota((256, 32), 0) // 8)
    row_f = iota((64, 256), 1) % 8
    row_t = iota((256, 128), 0) % 8
    half_t = iota((256, 128), 1) // 64

    def pick(gap, parts):
        return jnp.where(
            gap == 0, parts[0], jnp.where(gap == 1, parts[1], jnp.where(gap == 2, parts[2], 0.0))
        ).astype(BF16)

    def build(index, carry):
        a = index // 3
        e = index % 3
        taps = [wt[a, b, e] for b in range(3)]
        wide = [
            lax.dot_general(w, spread_t, (((0,), (0,)), ((), ())), preferred_element_type=F32)
            for w in taps
        ]
        for j in range(4):
            tf[index, 64 * j : 64 * j + 64, :] = pick(row_f - 2 * j + 1, wide)
        tall = [dot(spread, jnp.concatenate([w, w], axis=1)) for w in taps]
        for pair in range(3):
            j = 2 * pair + half_t
            gap = jnp.where(j > 4, 9, row_t - 2 * j + 1)
            tt[index, :, 128 * pair : 128 * pair + 128] = pick(gap, tall)
        return carry

    lax.fori_loop(0, 9, build, 0)
    m0[320:384, :] = jnp.zeros((64, 128), BF16)
    m1[320:384, :] = jnp.zeros((64, 128), BF16)

    def split(rows):
        return dot(rows, sel[...]).astype(BF16)

    def rows_of(ref):
        return ref[...].astype(F32).reshape(256, 256).astype(BF16)

    def body_taps(a, views):
        total = dot(tf[3 * a], views[:, 0:128])
        total = total + dot(tf[3 * a + 1], views[:, 128:256])
        return total + dot(tf[3 * a + 2], views[:, 256:384])

    def edge_taps(a, rows):
        views = split(rows)
        total = None
        for e in range(3):
            part = lax.dot_general(
                wt[a, 0, e], views[:, 128 * e : 128 * e + 128],
                (((0,), (0,)), ((), ())), preferred_element_type=F32,
            )
            total = part if total is None else total + part
        return total

    last_row = one_hot(iota((32, 256), 1) == 8 * iota((32, 256), 0) + 7)

    landed(rx1, X1)
    remote(rx1, rxh, XH, (above, me)).start()
    plane = rows_of(rx1)
    hs1[...] = dot(last_row, plane).astype(BF16)
    remote(hs1, h1, H1, (slab, after)).start()
    remote(hs1, hm, HM, (above, after)).start()
    pre = body_taps(2, split(plane))

    landed(rx0, X0)
    plane = rows_of(rx0)
    hs0[...] = dot(last_row, plane).astype(BF16)
    remote(hs0, h0, H0, (slab, after)).start()
    pre = pre + body_taps(1, split(plane))

    landed(brx, BS)
    owner = iota((64, 128), 0) // 4
    shown = jnp.zeros((64, 128), F32)
    for rank in range(ranks):
        shown = jnp.where(owner == rank, jnp.broadcast_to(brx[rank], (64, 128)), shown)
    mine = iota((64, 128), 1) == iota((64, 128), 0) % 4
    column = jnp.sum(jnp.where(mine, shown, 0.0), axis=1, keepdims=True)
    order = one_hot(frm == (to % 64) // 4 * 16 + (to // 64) * 4 + to % 4)
    landed(crx, CT)
    upstream = dot(order, crx[...].reshape(256, 128))

    landed(h1, H1)
    edge = edge_taps(2, h1[...]) + jnp.broadcast_to(column, (64, 128))
    landed(h0, H0)
    edge = edge + edge_taps(1, h0[...])
    landed(hm, HM)
    edge = edge + edge_taps(0, hm[...])
    landed(rxh, XH)
    pre = pre + body_taps(0, split(rows_of(rxh)))
    rest = jnp.broadcast_to(column, (64, 128))
    pre = pre + jnp.concatenate([edge, rest, rest, rest], axis=0)

    decay = jnp.exp(-jnp.abs(pre))
    out = (0.3 * pre + 0.7 * (jnp.maximum(pre, 0.0) + jnp.log1p(decay))).astype(BF16)
    gate = jnp.where(pre >= 0.0, 1.0, decay) / (1.0 + decay)
    masked = (upstream * (0.3 + 0.7 * gate)).astype(BF16)
    m0[0:256, :] = masked
    remote(m0.at[pl.ds(0, 256)], m1.at[pl.ds(0, 256)], M1, (below, me)).start()
    remote(m0.at[pl.ds(0, 64)], m1.at[pl.ds(256, 64)], N1, (below, before)).start()
    remote(m0.at[pl.ds(0, 64)], m0.at[pl.ds(256, 64)], N0, (slab, before)).start()

    order = one_hot(frm == (to // 4) % 4 * 64 + to // 16 * 4 + to % 4)
    outs[...] = dot(order, out).astype(BF16).reshape(ranks, 16, 128)
    scatter(OS, lambda peer: outs.at[peer], orx.at[block])

    weave = one_hot(frm // 2 + (frm % 2) * 128 == to)

    def woven(even, odd):
        both = jnp.concatenate([even.astype(BF16), odd.astype(BF16)], axis=1)
        return dot(both, weave).astype(BF16).reshape(ranks, 2, 8, 256)

    def moved(rows):
        return pltpu.roll(rows.astype(F32), 127, 1).astype(BF16)

    landed(m0.at[pl.ds(256, 64)], N0)
    here = m0[...]
    here_next = moved(here)
    tg0[...] = woven(dot(tt[4], here), dot(tt[5], here) + dot(tt[3], here_next))
    scatter(G0, lambda peer: tg0.at[peer], grad.at[:, 0, block])
    even = dot(tt[7], here)
    odd = dot(tt[8], here) + dot(tt[6], here_next)
    landed(m1.at[pl.ds(0, 256)], M1)
    landed(m1.at[pl.ds(256, 64)], N1)
    there = m1[...]
    tg1[...] = woven(even + dot(tt[1], there), odd + dot(tt[2], there) + dot(tt[0], moved(there)))
    scatter(G1, lambda peer: tg1.at[peer], grad.at[:, 1, block])

    landed(orx, OS)
    order = one_hot(frm == (to % 64) // 4 * 16 + (to % 4) * 4 + to // 64)
    act[...] = dot(order, orx[...].reshape(256, 128)).astype(BF16)

    others = pl.ds(0, ranks - 1)
    for ref, kind in (
        (rx1.at[others], X1), (rx0.at[others], X0), (crx.at[others], CT), (brx.at[others], BS),
        (outs.at[others], OS), (tg0.at[others], G0), (tg1.at[others], G1),
        (rx1, XH), (hs1, H1), (hs1, HM), (hs0, H0),
        (m0.at[pl.ds(0, 256)], M1), (m0.at[pl.ds(0, 64)], N1), (m0.at[pl.ds(0, 64)], N0),
    ):
        left(ref, kind)
    landed(grad.at[:, 0], G0)
    landed(grad.at[:, 1], G1)


def on_device(slabs, ranks, field, kernel, bias, cotangent):
    vmem = pl.BlockSpec(memory_space=pltpu.VMEM)
    call = pl.pallas_call(
        functools.partial(block_kernel, slabs, ranks),
        out_shape=(
            jax.ShapeDtypeStruct((256, 128), BF16),
            jax.ShapeDtypeStruct((2, 2, ranks, 8, 256), BF16),
        ),
        in_specs=[vmem] * 4,
        out_specs=(vmem, vmem),
        scratch_shapes=[
            pltpu.VMEM((ranks, 2, 8, 256), BF16),
            pltpu.VMEM((ranks, 2, 8, 256), BF16),
            pltpu.VMEM((ranks, 2, 8, 256), BF16),
            pltpu.VMEM((32, 256), BF16),
            pltpu.VMEM((32, 256), BF16),
            pltpu.VMEM((32, 256), BF16),
            pltpu.VMEM((32, 256), BF16),
            pltpu.VMEM((32, 256), BF16),
            pltpu.VMEM((ranks, 16, 128), BF16),
            pltpu.VMEM((ranks, 16, 128), BF16),
            pltpu.VMEM((1, 128), F32),
            pltpu.VMEM((ranks, 1, 128), F32),
            pltpu.VMEM((ranks, 16, 128), BF16),
            pltpu.VMEM((ranks, 16, 128), BF16),
            pltpu.VMEM((384, 128), BF16),
            pltpu.VMEM((384, 128), BF16),
            pltpu.VMEM((ranks, 2, 8, 256), BF16),
            pltpu.VMEM((ranks, 2, 8, 256), BF16),
            pltpu.VMEM((9, 256, 256), BF16),
            pltpu.VMEM((9, 256, 384), BF16),
            pltpu.VMEM((256, 384), BF16),
            pltpu.SemaphoreType.DMA((KINDS,)),
            pltpu.SemaphoreType.DMA((KINDS,)),
        ],
        compiler_params=pltpu.CompilerParams(collective_id=0, has_side_effects=True),
        name="row_blocks",
    )
    act, grad = call(
        field.reshape(2, 2, ranks, 8, 256),
        kernel.transpose(2, 3, 4, 1, 0),
        bias.reshape(1, 4),
        cotangent.reshape(256, 128),
    )
    return act.reshape(4, 1, 64, 128), grad.reshape(2, 2, 128, 256)


def solution(mesh):
    in_specs = (P("col", "gx", None, None), P(), P("col"), P("col", "gx", None, None))
    out_specs = (P("col", "gx", None, None), P("col", "gx", None, None))
    return jax.shard_map(
        functools.partial(on_device, mesh.shape["gx"], mesh.shape["col"]),
        mesh=mesh, in_specs=in_specs, out_specs=out_specs, check_vma=False,
    )
```

profile of v0, /device:TPU:4, one launch (start us, length us, event | category | flops | bytes accessed | tf_op | source)
XLA Modules:
  0.0 44.3 jit_solution(17433649542291764561)
XLA Ops:
  0.6 40.5 %row_blocks.1 = (bf16[256,128]{1,0:T(8,128)(2,1)}, bf16[2,2,16,8,256]{4,3,2,1,0:T(8,128)(2,1)}) custom-call(bf16[2,2,16,8,256]{4,3,2,1,0:T(8,128)(2,1)} %bitcast.8, bf16[3,3,3,32,64]{4,3,2,1,0:T(8,128)(2,1)} %bitcast.10, f32[1,4]{1,0:T(1,128)} %bitcast.13, bf16[256,128]{1,0:T(8,128)(2,1)} %bitcast.11), custom_call_target="tpu_custom_call" | custom-call | tf_op jit(solution)/shard_map/row_blocks/pallas_call | solution.py:280
  41.1 1.5 %copy.9 = bf16[4,1,64,128]{3,2,1,0:T(8,128)(2,1)} copy(bf16[4,1,64,128]{3,2,1,0:T(8,128)(2,1)} %bitcast.12) | data formatting | bytes 131072
  42.6 1.7 %copy.10 = bf16[2,2,128,256]{3,2,1,0:T(8,128)(2,1)} copy(bf16[2,2,128,256]{3,2,1,0:T(8,128)(2,1)} %bitcast.9) | data formatting | bytes 524288
where the time goes:
time: 44.4 us; the launch traced here: 44.3 us
  Pallas kernels  40.5 us (91%)
  local copies, waits for them, and re-layouts  3.14 us (7%)
  between operations  0.64 us (1%)
    pallas_call x1, Pallas kernels, on_device(): call(field.reshape(2, 2, ranks, 8, 256), kernel.transpose(2, 3, 4, 1, 0),...  40.5 us
    unnamed x2, local copies, waits for them, and re-layouts  3.14 us

commit v1 on v0

v1 whole, which is shorter than its diff:
```python
import functools

import jax
import jax.numpy as jnp
from jax import lax
from jax.experimental import pallas as pl
from jax.experimental.pallas import tpu as pltpu
from jax.sharding import PartitionSpec as P

F32 = jnp.float32
BF16 = jnp.bfloat16
MESH = pl.DeviceIdType.MESH

X1, X0, CT, BS, OS, G0, G1, XH, H1, HM, H0, L1, LM, L0, M1 = range(15)
KINDS = 15


def iota(shape, dim):
    return lax.broadcasted_iota(jnp.int32, shape, dim)


def one_hot(hit):
    return jnp.where(hit, 1.0, 0.0).astype(BF16)


def dot(a, b):
    return jnp.dot(a, b, preferred_element_type=F32)


def row_block(position, ranks):
    return position + (position // (ranks // 2)) * (3 * ranks // 2 - 1 - 2 * position)


def block_kernel(
    slabs, ranks,
    field, wt_hbm, bias_hbm, cot_hbm,
    orx, grad,
    rx1, rx0, rxh, h1, h0, hm, hs1, hs0,
    wt, bias, cot, cs, crx, bs, brx, outs, m0, m1, tg0, tg1,
    tf, tt, sel, send, recv, load,
):
    slab = lax.axis_index("gx")
    me = lax.axis_index("col")
    block = row_block(me, ranks)
    above = lax.rem(slab + 1, slabs)
    below = lax.rem(slab + slabs - 1, slabs)
    after = row_block(lax.rem(block + 1, ranks), ranks)
    before = row_block(lax.rem(block + ranks - 1, ranks), ranks)

    barrier = pltpu.get_barrier_semaphore()

    def peer_of(step):
        turn = step // 2
        z = me + ranks // 4 + (1 - 2 * (turn % 2)) * ((turn + 1) // 2)
        y = me // (ranks // 2) + 1 - step % 2
        return (z % (ranks // 2)) + (y % 2) * (ranks // 2)

    def greet(step, carry):
        peer = peer_of(step)
        pl.semaphore_signal(barrier, inc=1, device_id=(slab, peer), device_id_type=MESH)
        return carry

    lax.fori_loop(0, ranks - 1, greet, 0)
    for where in (
        (above, me), (below, me), (above, after), (below, before), (above, before), (below, after)
    ):
        pl.semaphore_signal(barrier, inc=1, device_id=where, device_id_type=MESH)

    def remote(src, dst, kind, where):
        return pltpu.make_async_remote_copy(
            src_ref=src, dst_ref=dst, send_sem=send.at[kind], recv_sem=recv.at[kind],
            device_id=where, device_id_type=MESH,
        )

    def landed(ref, kind):
        pltpu.make_async_copy(ref, ref, recv.at[kind]).wait()

    def left(ref, kind):
        pltpu.make_async_copy(ref, ref, send.at[kind]).wait()

    def scatter(kind, source, target):
        def one(step, carry):
            peer = peer_of(step)
            remote(source(peer), target, kind, (slab, peer)).start()
            return carry

        lax.fori_loop(0, ranks - 1, one, 0)
        pltpu.make_async_copy(source(me), target, recv.at[kind]).start()

    loads = [
        pltpu.make_async_copy(src, dst, load.at[slot])
        for slot, (src, dst) in enumerate(((cot_hbm, cot), (bias_hbm, bias), (wt_hbm, wt)))
    ]
    for copy in loads:
        copy.start()
    bs[...] = jnp.zeros(bs.shape, F32)

    pl.semaphore_wait(barrier, ranks - 1 + 6)

    scatter(X1, lambda peer: field.at[:, 1, row_block(peer, ranks)], rx1.at[me])
    scatter(X0, lambda peer: field.at[:, 0, row_block(peer, ranks)], rx0.at[me])

    to = iota((384, 256), 0)
    frm = iota((384, 256), 1)
    taken = to % 24
    wanted = (taken % 4) * 64 + (to // 24 * 4 + taken // 4) % 64
    order = one_hot((frm == wanted) & (taken < 20))
    loads[0].wait()
    cs[...] = dot(order, cot[...]).reshape(ranks, 24, 128).astype(BF16)
    scatter(CT, lambda peer: cs.at[row_block(peer, ranks)], crx.at[me])
    loads[1].wait()
    bs[0:1, 0:4] = bias[...]
    scatter(BS, lambda peer: bs, brx.at[me])

    to = iota((256, 256), 0)
    frm = iota((256, 256), 1)
    source_z = iota((256, 384), 0)
    tap = iota((256, 384), 1)
    sel[...] = one_hot(source_z == (2 * (tap % 128) + tap // 128 + 255) % 256)
    loads[2].wait()

    spread_t = one_hot(iota((32, 256), 0) == iota((32, 256), 1) // 8)
    spread = one_hot(iota((256, 32), 1) == iota((256, 32), 0) // 8)
    row_f = iota((64, 256), 1) % 8
    row_t = iota((256, 128), 0) % 8
    half_t = iota((256, 128), 1) // 64

    def pick(gap, parts):
        return jnp.where(
            gap == 0, parts[0], jnp.where(gap == 1, parts[1], jnp.where(gap == 2, parts[2], 0.0))
        ).astype(BF16)

    def build(index, carry):
        a = index // 3
        e = index % 3
        taps = [wt[a, b, e] for b in range(3)]
        wide = [
            lax.dot_general(w, spread_t, (((0,), (0,)), ((), ())), preferred_element_type=F32)
            for w in taps
        ]
        for j in range(5):
            tf[index, 64 * j : 64 * j + 64, :] = pick(row_f - 2 * j + 1, wide)
        tall = [dot(spread, jnp.concatenate([w, w], axis=1)) for w in taps]
        for pair in range(3):
            j = 2 * pair + half_t
            gap = jnp.where(j > 4, 9, row_t - 2 * j + 1)
            tt[index, :, 128 * pair : 128 * pair + 128] = pick(gap, tall)
        return carry

    lax.fori_loop(0, 9, build, 0)
    m0[320:384, :] = jnp.zeros((64, 128), BF16)
    m1[320:384, :] = jnp.zeros((64, 128), BF16)

    def split(rows):
        return dot(rows, sel[...]).astype(BF16)

    def rows_of(ref):
        return ref[...].astype(F32).reshape(256, 256).astype(BF16)

    def body_taps(a, views):
        total = dot(tf[3 * a], views[:, 0:128])
        total = total + dot(tf[3 * a + 1], views[:, 128:256])
        return total + dot(tf[3 * a + 2], views[:, 256:384])

    def edge_taps(a, rows, taps):
        views = split(rows)
        total = None
        for place, b in enumerate(taps):
            for e in range(3):
                part = lax.dot_general(
                    wt[a, b, e], views[32 * place : 32 * place + 32, 128 * e : 128 * e + 128],
                    (((0,), (0,)), ((), ())), preferred_element_type=F32,
                )
                total = part if total is None else total + part
        return total

    edge_row = iota((96, 256), 0)
    edges = one_hot(iota((96, 256), 1) == 8 * (edge_row % 32) + (edge_row // 32 + 7) % 8)
    low, high = pl.ds(0, 32), pl.ds(32, 64)

    landed(rx1, X1)
    remote(rx1, rxh, XH, (above, me)).start()
    plane = rows_of(rx1)
    hs1[...] = dot(edges, plane).astype(BF16)
    remote(hs1.at[low], hm.at[low], HM, (above, after)).start()
    remote(hs1.at[high], hm.at[high], LM, (above, before)).start()
    remote(hs1.at[low], h1.at[low], H1, (slab, after)).start()
    remote(hs1.at[high], h1.at[high], L1, (slab, before)).start()
    pre = body_taps(2, split(plane))

    landed(rx0, X0)
    plane = rows_of(rx0)
    hs0[...] = dot(edges, plane).astype(BF16)
    remote(hs0.at[low], h0.at[low], H0, (slab, after)).start()
    remote(hs0.at[high], h0.at[high], L0, (slab, before)).start()
    pre = pre + body_taps(1, split(plane))

    landed(brx, BS)
    owner = iota((64, 128), 0) // 4
    shown = jnp.zeros((64, 128), F32)
    for rank in range(ranks):
        shown = jnp.where(owner == rank, jnp.broadcast_to(brx[rank], (64, 128)), shown)
    mine = iota((64, 128), 1) == iota((64, 128), 0) % 4
    column = jnp.sum(jnp.where(mine, shown, 0.0), axis=1, keepdims=True)
    dest = iota((320, 384), 0)
    order = one_hot(iota((320, 384), 1) == dest % 64 // 4 * 24 + dest // 64 * 4 + dest % 4)
    landed(crx, CT)
    upstream = dot(order, crx[...].astype(F32).reshape(24 * ranks, 128).astype(BF16))

    rest = jnp.broadcast_to(column, (64, 128))
    first, last = rest, rest
    for ref, a, kinds in ((h1, 2, (H1, L1)), (h0, 1, (H0, L0)), (hm, 0, (HM, LM))):
        landed(ref.at[low], kinds[0])
        landed(ref.at[high], kinds[1])
        first = first + edge_taps(a, ref[0:32, :], (0,))
        last = last + edge_taps(a, ref[32:96, :], (1, 2))
    landed(rxh, XH)
    pre = pre + body_taps(0, split(rows_of(rxh)))
    pre = pre + jnp.concatenate([first, rest, rest, rest, last], axis=0)

    decay = jnp.exp(-jnp.abs(pre))
    out = (0.3 * pre + 0.7 * (jnp.maximum(pre, 0.0) + jnp.log1p(decay))).astype(BF16)
    gate = jnp.where(pre >= 0.0, 1.0, decay) / (1.0 + decay)
    masked = (upstream * (0.3 + 0.7 * gate)).astype(BF16)
    m0[0:320, :] = masked
    whole = pl.ds(0, 320)
    remote(m0.at[whole], m1.at[whole], M1, (below, me)).start()

    weave = one_hot(frm // 2 + (frm % 2) * 128 == to)

    def woven(even, odd):
        both = jnp.concatenate([even.astype(BF16), odd.astype(BF16)], axis=1)
        return dot(both, weave).astype(BF16).reshape(ranks, 2, 8, 256)

    def moved(rows):
        return pltpu.roll(rows.astype(F32), 127, 1).astype(BF16)

    here = m0[...]
    here_next = moved(here)
    tg0[...] = woven(dot(tt[4], here), dot(tt[5], here) + dot(tt[3], here_next))
    scatter(G0, lambda peer: tg0.at[peer], grad.at[:, 0, block])
    order = one_hot(frm == (to // 4) % 4 * 64 + to // 16 * 4 + to % 4)
    outs[...] = dot(order, out[0:256]).astype(BF16).reshape(ranks, 16, 128)
    scatter(OS, lambda peer: outs.at[peer], orx.at[block])

    even = dot(tt[7], here)
    odd = dot(tt[8], here) + dot(tt[6], here_next)
    landed(m1.at[whole], M1)
    there = m1[...]
    tg1[...] = woven(even + dot(tt[1], there), odd + dot(tt[2], there) + dot(tt[0], moved(there)))
    scatter(G1, lambda peer: tg1.at[peer], grad.at[:, 1, block])

    others = pl.ds(0, ranks - 1)
    for ref, kind in (
        (rx1.at[others], X1), (rx0.at[others], X0), (crx.at[others], CT), (brx.at[others], BS),
        (outs.at[others], OS), (tg0.at[others], G0), (tg1.at[others], G1),
        (rx1, XH), (hs1.at[low], H1), (hs1.at[low], HM), (hs0.at[low], H0),
        (hs1.at[high], L1), (hs1.at[high], LM), (hs0.at[high], L0), (m0.at[whole], M1),
    ):
        left(ref, kind)
    landed(orx, OS)
    landed(grad.at[:, 0], G0)
    landed(grad.at[:, 1], G1)


def leave_kernel(orx_hbm, grad_hbm, act_out, grad_out, orx, act, grad, sems):
    reads = [pltpu.make_async_copy(orx_hbm, orx, sems.at[0])]
    writes = []
    for half in range(2):
        reads.append(pltpu.make_async_copy(grad_hbm.at[half], grad.at[half], sems.at[1 + half]))
        writes.append(pltpu.make_async_copy(grad.at[half], grad_out.at[half], sems.at[3 + half]))
    for copy in reads:
        copy.start()
    to = iota((256, 256), 0)
    order = one_hot(iota((256, 256), 1) == (to % 64) // 4 * 16 + (to % 4) * 4 + to // 64)
    reads[0].wait()
    act[...] = dot(order, orx[...].reshape(256, 128)).astype(BF16)
    last = pltpu.make_async_copy(act, act_out, sems.at[5])
    last.start()
    for half in range(2):
        reads[1 + half].wait()
        writes[half].start()
    for copy in writes:
        copy.wait()
    last.wait()


def on_device(slabs, ranks, field, kernel, bias, cotangent):
    where = pl.BlockSpec(memory_space=pl.ANY)
    block = pltpu.VMEM((ranks, 2, 8, 256), BF16)
    edge = pltpu.VMEM((96, 256), BF16)
    act_shape = jax.ShapeDtypeStruct((ranks, 16, 128), BF16)
    grad_shape = jax.ShapeDtypeStruct((2, 2, ranks, 8, 256), BF16)
    call = pl.pallas_call(
        functools.partial(block_kernel, slabs, ranks),
        out_shape=(act_shape, grad_shape),
        in_specs=[where] * 4,
        out_specs=(where, where),
        scratch_shapes=[
            block, block, block,
            edge, edge, edge, edge, edge,
            pltpu.VMEM((3, 3, 3, 32, 64), BF16),
            pltpu.VMEM((1, 4), F32),
            pltpu.VMEM((256, 128), BF16),
            pltpu.VMEM((ranks, 24, 128), BF16),
            pltpu.VMEM((ranks, 24, 128), BF16),
            pltpu.VMEM((1, 128), F32),
            pltpu.VMEM((ranks, 1, 128), F32),
            pltpu.VMEM((ranks, 16, 128), BF16),
            pltpu.VMEM((384, 128), BF16),
            pltpu.VMEM((384, 128), BF16),
            block, block,
            pltpu.VMEM((9, 320, 256), BF16),
            pltpu.VMEM((9, 256, 384), BF16),
            pltpu.VMEM((256, 384), BF16),
            pltpu.SemaphoreType.DMA((KINDS,)),
            pltpu.SemaphoreType.DMA((KINDS,)),
            pltpu.SemaphoreType.DMA((3,)),
        ],
        compiler_params=pltpu.CompilerParams(collective_id=0, has_side_effects=True),
        name="row_blocks",
    )
    orx, grad = call(
        field.reshape(2, 2, ranks, 8, 256),
        kernel.transpose(2, 3, 4, 1, 0),
        bias.reshape(1, 4),
        cotangent.reshape(256, 128),
    )
    leave = pl.pallas_call(
        leave_kernel,
        out_shape=(jax.ShapeDtypeStruct((256, 128), BF16), grad_shape),
        in_specs=[where] * 2,
        out_specs=(where, where),
        scratch_shapes=[
            pltpu.VMEM((ranks, 16, 128), BF16),
            pltpu.VMEM((256, 128), BF16),
            pltpu.VMEM((2, 2, ranks, 8, 256), BF16),
            pltpu.SemaphoreType.DMA((6,)),
        ],
        name="leave",
    )
    act, grad = leave(orx, grad)
    return act.reshape(4, 1, 64, 128), grad.reshape(2, 2, 128, 256)


def solution(mesh):
    in_specs = (P("col", "gx", None, None), P(), P("col"), P("col", "gx", None, None))
    out_specs = (P("col", "gx", None, None), P("col", "gx", None, None))
    return jax.shard_map(
        functools.partial(on_device, mesh.shape["gx"], mesh.shape["col"]),
        mesh=mesh, in_specs=in_specs, out_specs=out_specs, check_vma=False,
    )
```

time: 44.4 us -> 39.1 us (0.88)
  the two profiles are of different devices: /device:TPU:4 before, /device:TPU:1 now
where the time goes in v1:
time: 39.1 us; the launch traced here: 39 us
  Pallas kernels  38.4 us (98%)
  between operations  0.64 us (2%)
    pallas_call x1, Pallas kernels, on_device(): call(field.reshape(2, 2, ranks, 8, 256), kernel.transpose(2, 3, 4, 1, 0),...  36.6 us
    pallas_call x1, Pallas kernels, on_device(): act, grad = leave(orx, grad)  1.79 us

profile of v1, /device:TPU:1, one launch (start us, length us, event | category | flops | bytes accessed | tf_op | source)
XLA Modules:
  0.0 39.0 jit_solution(6628526020830532017)
XLA Ops:
  0.6 36.6 %row_blocks.1 = (bf16[16,16,128]{2,1,0:T(8,128)(2,1)}, bf16[2,2,16,8,256]{4,3,2,1,0:T(8,128)(2,1)}) custom-call(bf16[2,2,16,8,256]{4,3,2,1,0:T(8,128)(2,1)} %bitcast.8, bf16[3,3,3,32,64]{4,3,2,1,0:T(8,128)(2,1)} %bitcast.9, f32[1,4]{1,0:T(1,128)} %bitcast.11, bf16[256,128]{1,0:T(8,128)(2,1)} %bitcast.10), custom_call_target="tpu_custom_call" | custom-call | tf_op jit(solution)/shard_map/row_blocks/pallas_call | solution.py:323
  37.2 1.8 %leave.1 = (bf16[256,128]{1,0:T(8,128)(2,1)}, bf16[2,2,16,8,256]{4,3,2,1,0:T(8,128)(2,1)}) custom-call(bf16[16,16,128]{2,1,0:T(8,128)(2,1)} %get-tuple-element.6.orx_hbm, bf16[2,2,16,8,256]{4,3,2,1,0:T(8,128)(2,1)} %get-tuple-element.7.grad_hbm), custom_call_target="tpu_custom_call" | custom-call | tf_op jit(solution)/shard_map/leave/pallas_call | solution.py:342
